TPU v7x, 256 devices: a whole 4x4x8 slice. The times are simulated.
256 devices in a mesh: row: 8 (over x, core), col: 32 (over y, z).
Axes of the slice: x: 4, y: 4, z: 8, core: 2. Of those that a mesh axis runs over, the one named last changes fastest.
Arguments:
- inv_diag: float32 [2, 2048, 2048], P(None, 'row', 'col'), may hold values from -1 to 2, as said below
- coupling: float32 [2048, 2048], P('row', 'col'), may hold values from -0.125 to 0.125
- top_rhs: float32 [2, 2048, 4096], P(None, 'row', 'col'), may hold values from -6 to 6
- panel: float32 [2, 8192, 2048], P(None, 'row', 'col'), may hold values from -0.125 to 0.125
- rhs: float32 [8192, 4096], P('row', 'col'), may hold values from -6 to 6
Outputs:
- solved: float32 [2, 2048, 4096], P(None, 'row', 'col')
- trailing: float32 [8192, 4096], P('row', 'col')
Inputs may be any that keep to these rules, and one draw needn't show every extreme that they name: `inv_diag`: each of the two blocks is lower triangular with its diagonal in 1 to 2.
All inputs are finite; a program needn't handle non-finite values.
Results may differ from a plain program's by a relative error of at most 0.000073.
Values sent between devices are 32-bit elements; how exact they have to be, the bound alone decides.
A program may use at most 64 MiB of HBM per device.

v0:
```python
import jax
import jax.numpy as jnp
from jax import lax
from jax.sharding import PartitionSpec as P


def product(left, right):
    return jnp.dot(left, right, precision=lax.Precision.HIGHEST, preferred_element_type=jnp.float32)


def folder(full_rows, piece):
    return product(piece, full_rows)


def body(inv_diag, coupling, top_rhs, panel, rhs):
    first_full_rhs = lax.all_gather(top_rhs[0], "row", axis=0, tiled=True)
    solved_one = folder(first_full_rhs, lax.all_gather(inv_diag[0], "col", axis=1, tiled=True))
    full_one = lax.all_gather(solved_one, "row", axis=0, tiled=True)
    reduced = top_rhs[1] - folder(full_one, lax.all_gather(coupling, "col", axis=1, tiled=True))
    reduced_full = lax.all_gather(reduced, "row", axis=0, tiled=True)
    solved_two = folder(reduced_full, lax.all_gather(inv_diag[1], "col", axis=1, tiled=True))
    full_two = lax.all_gather(solved_two, "row", axis=0, tiled=True)
    solved = jnp.stack([solved_one, solved_two])
    stacked_full = jnp.stack([full_one, full_two])
    update = jnp.einsum(
        "krw,kwt->rt",
        lax.all_gather(panel, "col", axis=2, tiled=True),
        stacked_full,
        precision=lax.Precision.HIGHEST,
        preferred_element_type=jnp.float32,
    )
    trailing = rhs - update
    return (solved, trailing)


def solution(mesh):
    in_specs = (
        P(None, "row", "col"),
        P("row", "col"),
        P(None, "row", "col"),
        P(None, "row", "col"),
        P("row", "col"),
    )
    out_specs = (P(None, "row", "col"), P("row", "col"))
    return jax.shard_map(body, mesh=mesh, in_specs=in_specs, out_specs=out_specs, check_vma=False)
```

profile of v0, /device:TPU:1, one launch (start us, length us, event | category | flops | bytes accessed | tf_op | source)
XLA Modules:
  0.0 524.7 jit_solution(6172325524292058646)
XLA Ops:
  7.2 0.0 copy-start.3
  7.2 0.0 all-gather.24.cloned.1.call-start
  7.2 1.6 slice.13
  8.8 0.0 all-gather.24.cloned.1.call-update
  8.8 0.0 all-gather.22.cloned.1.call-start
  8.9 1.5 fusion.17
  10.4 0.0 all-gather.22.cloned.1.call-update
  10.4 0.0 all-gather.14.cloned.1.call-start
  10.5 0.7 all-gather.14.cloned.1.call-update
  11.2 0.0 all-gather.12.cloned.1.call-start
  11.2 29.2 %all-gather.24.cloned.1.call-done = f32[1,2048,128]{2,1,0:T(8,128)} async-done(((f32[1,256,128]{2,1,0:T(8,128)}), f32[1,2048,128]{2,1,0:T(8,128)}) %all-gather.24.cloned.1.call-update) | async-done | bytes 1048592 | tf_op jit(solution)/shard_map/all_gather | solution.py:16
  40.4 76.0 %all-gather.22.cloned.1.call-done = f32[1,256,2048]{1,2,0:T(8,128)} async-done(((f32[1,256,64]{1,2,0:T(8,128)}), f32[1,256,2048]{1,2,0:T(8,128)}) %all-gather.22.cloned.1.call-update) | async-done | bytes 2097168 | tf_op jit(solution)/shard_map/all_gather | solution.py:17
  116.4 5.9 %fusion.6 = f32[256,128]{1,0:T(8,128)} fusion(f32[1,256,2048]{1,2,0:T(8,128)} %all-gather.22.cloned.1.call-done, f32[1,2048,128]{2,1,0:T(8,128)} %all-gather.24.cloned.1.call-done), kind=kOutput, calls=%fused_computation.6 | convolution fusion | flops 805306368 | bytes 3276800 | tf_op jit(solution)/shard_map/dot_general | solution.py:8
  122.4 0.0 all-gather.12.cloned.1.call-update
  122.4 0.0 all-gather.26.cloned.1.call-start
  122.4 0.5 all-gather.26.cloned.1.call-update
  123.0 0.0 all-gather.16.cloned.1.call-start
  123.0 71.2 %all-gather.14.cloned.1.call-done = f32[256,2048]{0,1:T(8,128)} async-done(((f32[256,64]{0,1:T(8,128)}), f32[256,2048]{0,1:T(8,128)}) %all-gather.14.cloned.1.call-update) | async-done | bytes 2097168 | tf_op jit(solution)/shard_map/all_gather | solution.py:19
  194.2 30.3 %all-gather.12.cloned.1.call-done = f32[2048,128]{1,0:T(8,128)} async-done(((f32[256,128]{1,0:T(8,128)}), f32[2048,128]{1,0:T(8,128)}) %all-gather.12.cloned.1.call-update) | async-done | bytes 1048592 | tf_op jit(solution)/shard_map/all_gather | solution.py:18
  224.5 0.0 copy-done.3
  224.5 6.0 %fusion.14 = f32[256,128]{1,0:T(8,128)} fusion(f32[2048,128]{1,0:T(8,128)} %all-gather.12.cloned.1.call-done, f32[256,2048]{0,1:T(8,128)} %all-gather.14.cloned.1.call-done, f32[2,256,128]{2,1,0:T(8,128)S(1)} %copy-done.3), kind=kOutput, calls=%fused_computation.11 | convolution fusion | flops 805339136 | bytes 3407872 | tf_op jit(solution)/shard_map/dot_general | solution.py:8
  230.5 0.0 copy-start.2
  230.5 0.0 all-gather.16.cloned.1.call-update
  230.5 0.0 copy-start.1
  230.5 0.0 copy-start
  230.5 0.0 all-gather.18.cloned.1.call-start
  230.6 69.2 %all-gather.26.cloned.1.call-done = f32[1,256,2048]{1,2,0:T(8,128)} async-done(((f32[1,256,64]{1,2,0:T(8,128)}), f32[1,256,2048]{1,2,0:T(8,128)}) %all-gather.26.cloned.1.call-update) | async-done | bytes 2097168 | tf_op jit(solution)/shard_map/all_gather | solution.py:21
  299.8 30.3 %all-gather.16.cloned.1.call-done = f32[2048,128]{1,0:T(8,128)} async-done(((f32[256,128]{1,0:T(8,128)}), f32[2048,128]{1,0:T(8,128)}) %all-gather.16.cloned.1.call-update) | async-done | bytes 1048592 | tf_op jit(solution)/shard_map/all_gather | solution.py:20
  330.1 6.0 %fusion.4 = f32[128,256]{0,1:T(8,128)} fusion(f32[2048,128]{1,0:T(8,128)} %all-gather.16.cloned.1.call-done, f32[1,256,2048]{1,2,0:T(8,128)} %all-gather.26.cloned.1.call-done), kind=kOutput, calls=%fused_computation.4 | convolution fusion | flops 805306368 | bytes 3276800 | tf_op jit(solution)/shard_map/dot_general | solution.py:8
  336.1 0.0 all-gather.18.cloned.1.call-update
  336.1 0.2 all-gather.20.cloned.1.call-start
  336.3 0.5 all-gather.20.cloned.1.call-update
  336.9 0.0 copy-done.2
  336.9 0.2 copy.9
  337.1 0.0 copy-done.1
  337.1 1.6 pad_maximum_fusion
  338.7 23.2 %all-gather.18.cloned.1.call-done = f32[2048,128]{1,0:T(8,128)} async-done(((f32[256,128]{1,0:T(8,128)}), f32[2048,128]{1,0:T(8,128)}) %all-gather.18.cloned.1.call-update) | async-done | bytes 1048592 | tf_op jit(solution)/shard_map/all_gather | solution.py:22
  361.9 141.1 %all-gather.20.cloned.1.call-done = f32[2,1024,2048]{1,2,0:T(8,128)} async-done(((f32[2,1024,64]{1,2,0:T(8,128)}), f32[2,1024,2048]{1,2,0:T(8,128)}) %all-gather.20.cloned.1.call-update) | async-done | bytes 16777232 | tf_op jit(solution)/shard_map/all_gather | solution.py:27
  503.0 0.0 copy-done
  503.0 13.8 %fusion.11 = f32[1024,128]{0,1:T(8,128)S(1)} fusion(f32[1024,128]{0,1:T(8,128)S(1)} %copy.9, f32[2,1024,2048]{1,2,0:T(8,128)} %all-gather.20.cloned.1.call-done, f32[1,2048,128]{2,1,0:T(8,128)} %bitcast.35, f32[1,2048,128]{2,1,0:T(8,128)S(1)} %bitcast.31), kind=kOutput, calls=%fused_computation.9 | convolution fusion | flops 6443106304 | bytes 19922944 | tf_op jit(solution)/shard_map/krw,kwt->rt/dot_general | solution.py:25
  516.9 1.0 copy.10
Async XLA Ops:
  7.2 217.3 %copy-start.3 = (f32[2,256,128]{2,1,0:T(8,128)S(1)}, f32[2,256,128]{2,1,0:T(8,128)}, u32[]{:S(2)}) copy-start(f32[2,256,128]{2,1,0:T(8,128)} %param.7) | copy-start | bytes 786436
  7.2 33.2 %all-gather.24.cloned.1.call-start = ((), (), s32[]{:S(2)}) async-start(), calls=%async_computation.6 | async-start | bytes 1179648 | tf_op jit(solution)/shard_map/all_gather | solution.py:16
  8.8 107.6 %all-gather.22.cloned.1.call-start = ((), (), s32[]{:S(2)}) async-start(), calls=%async_computation.5 | async-start | bytes 2162688 | tf_op jit(solution)/shard_map/all_gather | solution.py:17
  10.4 183.7 %all-gather.14.cloned.1.call-start = ((), (), s32[]{:S(2)}) async-start(), calls=%async_computation.1 | async-start | bytes 2162688 | tf_op jit(solution)/shard_map/all_gather | solution.py:19
  11.2 213.3 %all-gather.12.cloned.1.call-start = ((), (), s32[]{:S(2)}) async-start(), calls=%async_computation | async-start | bytes 1179648 | tf_op jit(solution)/shard_map/all_gather | solution.py:18
  122.4 177.4 %all-gather.26.cloned.1.call-start = ((), (), s32[]{:S(2)}) async-start(), calls=%async_computation.7 | async-start | bytes 2162688 | tf_op jit(solution)/shard_map/all_gather | solution.py:21
  123.0 207.1 %all-gather.16.cloned.1.call-start = ((), (), s32[]{:S(2)}) async-start(), calls=%async_computation.2 | async-start | bytes 1179648 | tf_op jit(solution)/shard_map/all_gather | solution.py:20
  230.5 106.4 %copy-start.2 = (f32[1024,128]{1,0:T(8,128)S(1)}, f32[1024,128]{1,0:T(8,128)}, u32[]{:S(2)}) copy-start(f32[1024,128]{1,0:T(8,128)} %param.9) | copy-start | bytes 1572868
  230.5 106.6 %copy-start.1 = (f32[256,128]{1,0:T(8,128)S(1)}, f32[256,128]{1,0:T(8,128)}, u32[]{:S(2)}) copy-start(f32[256,128]{1,0:T(8,128)} %fusion.6) | copy-start | bytes 393220
  230.5 272.5 %copy-start = (f32[2048,128]{1,0:T(8,128)S(1)}, f32[2048,128]{1,0:T(8,128)}, u32[]{:S(2)}) copy-start(f32[2048,128]{1,0:T(8,128)} %all-gather.12.cloned.1.call-done) | copy-start | bytes 3145732
  230.5 131.4 %all-gather.18.cloned.1.call-start = ((), (), s32[]{:S(2)}) async-start(), calls=%async_computation.3 | async-start | bytes 1179648 | tf_op jit(solution)/shard_map/all_gather | solution.py:22
  336.1 166.9 %all-gather.20.cloned.1.call-start = ((), (), s32[]{:S(2)}) async-start(), calls=%async_computation.4 | async-start | bytes 17301504 | tf_op jit(solution)/shard_map/all_gather | solution.py:27
Sparse Core Ops, SparseCore 0:
  10.4 29.9 all-gather.23
  43.6 72.8 all-gather.21
  119.0 75.1 all-gather.13
  196.5 27.9 all-gather.11
  226.9 72.8 all-gather.25
  302.1 27.9 all-gather.15
  336.2 25.6 all-gather.17
  364.5 138.4 all-gather.19
where the time goes:
time: 525 us
  waiting for transfers between devices  472 us (90%)
  matrix products  31.8 us (6%)
  between operations  14.2 us (3%)
    all_gather x1, waiting for transfers between devices, body(): lax.all_gather(panel, 'col', axis=2, tiled=True)  141 us
    all_gather x1, waiting for transfers between devices, body(): lax.all_gather(inv_diag[0], 'col', axis=1, tiled=True)  76 us
    all_gather x1, waiting for transfers between devices, body(): lax.all_gather(coupling, 'col', axis=1, tiled=True)  71.2 us
    all_gather x1, waiting for transfers between devices, body(): lax.all_gather(inv_diag[1], 'col', axis=1, tiled=True)  69.2 us
    all_gather x1, waiting for transfers between devices, body(): full_one = lax.all_gather(solved_one, 'row', axis=0, tiled=True)  30.3 us
    all_gather x1, waiting for transfers between devices, body(): reduced_full = lax.all_gather(reduced, 'row', axis=0, tiled=True)  30.3 us
    all_gather x1, waiting for transfers between devices, body(): first_full_rhs = lax.all_gather(top_rhs[0], 'row', axis=0, tiled=True)  29.2 us
    all_gather x1, waiting for transfers between devices, body(): full_two = lax.all_gather(solved_two, 'row', axis=0, tiled=True)  23.2 us
  transfers between devices with their start and end apart: 8, of which 8 were waited for; matrix products, arithmetic and copies ran while one was open for 3% of the time, Pallas kernels for 0%

commit v1 on v0

--- a/solution.py
+++ b/solution.py
@@ -17,7 +17,9 @@
     solved_one = folder(first_full_rhs, lax.all_gather(inv_diag[0], "col", axis=1, tiled=True))
     full_one = lax.all_gather(solved_one, "row", axis=0, tiled=True)
     reduced = top_rhs[1] - folder(full_one, lax.all_gather(coupling, "col", axis=1, tiled=True))
-    reduced_full = lax.all_gather(reduced, "row", axis=0, tiled=True)
+    reduced_full = jnp.concatenate(
+        lax.all_to_all(jnp.stack([reduced] * lax.axis_size("row")), "row", 0, 0), axis=0
+    )
     solved_two = folder(reduced_full, lax.all_gather(inv_diag[1], "col", axis=1, tiled=True))
     full_two = lax.all_gather(solved_two, "row", axis=0, tiled=True)
     solved = jnp.stack([solved_one, solved_two])

time: 525 us -> 497 us (0.947)
  waiting for transfers between devices: 472 us -> 442 us
    all_gather x1 -> x0, waiting for transfers between devices: 30.3 us -> none  [body(): reduced_full = lax.all_gather(reduced, 'row', axis=0, tiled=True)]
  transfers between devices with their start and end apart: 8 -> 8, of which waited for: 8 -> 7; matrix products, arithmetic and copies ran while one was open for 3% -> 3% of each run, Pallas kernels for 0% -> 0%
where the time goes in v1:
time: 497 us
  waiting for transfers between devices  442 us (89%)
  matrix products  29.3 us (6%)
  between operations  14.2 us (3%)
  local copies, waits for them, and re-layouts  5.63 us (1%)
    all_gather x1, waiting for transfers between devices, body(): lax.all_gather(panel, 'col', axis=2, tiled=True)  141 us
    all_gather x1, waiting for transfers between devices, body(): lax.all_gather(inv_diag[0], 'col', axis=1, tiled=True)  75.5 us
    all_gather x1, waiting for transfers between devices, body(): lax.all_gather(coupling, 'col', axis=1, tiled=True)  71.1 us
    all_gather x1, waiting for transfers between devices, body(): lax.all_gather(inv_diag[1], 'col', axis=1, tiled=True)  67.2 us
    all_gather x1, waiting for transfers between devices, body(): full_one = lax.all_gather(solved_one, 'row', axis=0, tiled=True)  30.3 us
    all_gather x1, waiting for transfers between devices, body(): first_full_rhs = lax.all_gather(top_rhs[0], 'row', axis=0, tiled=True)  29.1 us
    all_gather x1, waiting for transfers between devices, body(): full_two = lax.all_gather(solved_two, 'row', axis=0, tiled=True)  25.5 us
    dot_general x3, matrix products, product(): jnp.dot(left, right, precision=lax.Precision.HIGHEST, preferred_element_t...  15.5 us
  transfers between devices with their start and end apart: 8, of which 7 were waited for; matrix products, arithmetic and copies ran while one was open for 3% of the time, Pallas kernels for 0%

profile of v1, /device:TPU:1, one launch (start us, length us, event | category | flops | bytes accessed | tf_op | source)
XLA Modules:
  0.0 496.5 jit_solution(9042975663062007161)
XLA Ops:
  7.2 0.0 all-gather.21.cloned.1.call-start
  7.2 1.6 fusion.17
  8.9 0.0 all-gather.21.cloned.1.call-update
  8.9 0.0 all-gather.19.cloned.1.call-start
  8.9 1.5 fusion.18
  10.4 0.0 all-gather.19.cloned.1.call-update
  10.5 0.0 all-gather.13.cloned.1.call-start
  10.5 0.7 all-gather.13.cloned.1.call-update
  11.2 0.0 all-gather.11.cloned.1.call-start
  11.3 29.1 %all-gather.21.cloned.1.call-done = f32[1,2048,128]{2,1,0:T(8,128)} async-done(((f32[1,256,128]{2,1,0:T(8,128)}), f32[1,2048,128]{2,1,0:T(8,128)}) %all-gather.21.cloned.1.call-update) | async-done | bytes 1048592 | tf_op jit(solution)/shard_map/all_gather | solution.py:16
  40.4 75.5 %all-gather.19.cloned.1.call-done = f32[1,256,2048]{1,2,0:T(8,128)} async-done(((f32[1,256,64]{1,2,0:T(8,128)}), f32[1,256,2048]{1,2,0:T(8,128)}) %all-gather.19.cloned.1.call-update) | async-done | bytes 2097168 | tf_op jit(solution)/shard_map/all_gather | solution.py:17
  115.8 5.9 %fusion.6 = f32[256,128]{1,0:T(8,128)} fusion(f32[1,256,2048]{1,2,0:T(8,128)} %all-gather.19.cloned.1.call-done, f32[1,2048,128]{2,1,0:T(8,128)} %all-gather.21.cloned.1.call-done), kind=kOutput, calls=%fused_computation.6 | convolution fusion | flops 805306368 | bytes 3276800 | tf_op jit(solution)/shard_map/dot_general | solution.py:8
  121.8 0.0 all-gather.11.cloned.1.call-update
  121.8 0.0 all-gather.23.cloned.1.call-start
  121.8 0.5 all-gather.23.cloned.1.call-update
  122.4 0.1 copy.15
  122.5 71.1 %all-gather.13.cloned.1.call-done = f32[256,2048]{0,1:T(8,128)} async-done(((f32[256,64]{0,1:T(8,128)}), f32[256,2048]{0,1:T(8,128)}) %all-gather.13.cloned.1.call-update) | async-done | bytes 2097168 | tf_op jit(solution)/shard_map/all_gather | solution.py:19
  193.6 30.3 %all-gather.11.cloned.1.call-done = f32[2048,128]{1,0:T(8,128)} async-done(((f32[256,128]{1,0:T(8,128)}), f32[2048,128]{1,0:T(8,128)}) %all-gather.11.cloned.1.call-update) | async-done | bytes 1048592 | tf_op jit(solution)/shard_map/all_gather | solution.py:18
  223.9 3.8 fusion.14
  227.7 0.1 copy.8
  227.8 1.1 stack.30
  228.9 3.7 all-to-all-start
  232.6 0.0 copy-start.2
  232.6 0.0 all-gather.15.cloned.1.call-start
  232.6 67.2 %all-gather.23.cloned.1.call-done = f32[1,256,2048]{1,2,0:T(8,128)} async-done(((f32[1,256,64]{1,2,0:T(8,128)}), f32[1,256,2048]{1,2,0:T(8,128)}) %all-gather.23.cloned.1.call-update) | async-done | bytes 2097168 | tf_op jit(solution)/shard_map/all_gather | solution.py:23
  299.8 0.0 all-to-all-done
  299.8 0.0 copy-start.1
  299.8 0.0 copy-start
  299.8 5.8 %fusion.4 = f32[128,256]{0,1:T(8,128)} fusion(f32[2048,128]{1,0:T(8,128)S(1)} %bitcast.33, f32[1,256,2048]{1,2,0:T(8,128)} %all-gather.23.cloned.1.call-done), kind=kOutput, calls=%fused_computation.4 | convolution fusion | flops 805306368 | bytes 3276800 | tf_op jit(solution)/shard_map/dot_general | solution.py:8
  305.6 0.0 all-gather.15.cloned.1.call-update
  305.6 0.2 all-gather.17.cloned.1.call-start
  305.8 0.5 all-gather.17.cloned.1.call-update
  306.3 0.0 copy-done.2
  306.3 0.2 copy.11
  306.5 0.0 copy-done.1
  306.6 1.6 pad_maximum_fusion
  308.2 25.5 %all-gather.15.cloned.1.call-done = f32[2048,128]{1,0:T(8,128)} async-done(((f32[256,128]{1,0:T(8,128)}), f32[2048,128]{1,0:T(8,128)}) %all-gather.15.cloned.1.call-update) | async-done | bytes 1048592 | tf_op jit(solution)/shard_map/all_gather | solution.py:24
  333.7 141.1 %all-gather.17.cloned.1.call-done = f32[2,1024,2048]{1,2,0:T(8,128)} async-done(((f32[2,1024,64]{1,2,0:T(8,128)}), f32[2,1024,2048]{1,2,0:T(8,128)}) %all-gather.17.cloned.1.call-update) | async-done | bytes 16777232 | tf_op jit(solution)/shard_map/all_gather | solution.py:29
  474.8 0.0 copy-done
  474.8 13.8 %fusion.11 = f32[1024,128]{0,1:T(8,128)S(1)} fusion(f32[1024,128]{0,1:T(8,128)S(1)} %copy.11, f32[2,1024,2048]{1,2,0:T(8,128)} %all-gather.17.cloned.1.call-done, f32[1,2048,128]{2,1,0:T(8,128)} %bitcast.37, f32[1,2048,128]{2,1,0:T(8,128)S(1)} %bitcast.32), kind=kOutput, calls=%fused_computation.9 | convolution fusion | flops 6443106304 | bytes 19922944 | tf_op jit(solution)/shard_map/krw,kwt->rt/dot_general | solution.py:27
  488.7 1.0 copy.12
Async XLA Ops:
  7.2 33.2 %all-gather.21.cloned.1.call-start = ((), (), s32[]{:S(2)}) async-start(), calls=%async_computation.6 | async-start | bytes 1179648 | tf_op jit(solution)/shard_map/all_gather | solution.py:16
  8.9 107.0 %all-gather.19.cloned.1.call-start = ((), (), s32[]{:S(2)}) async-start(), calls=%async_computation.5 | async-start | bytes 2162688 | tf_op jit(solution)/shard_map/all_gather | solution.py:17
  10.5 183.1 %all-gather.13.cloned.1.call-start = ((), (), s32[]{:S(2)}) async-start(), calls=%async_computation.2 | async-start | bytes 2162688 | tf_op jit(solution)/shard_map/all_gather | solution.py:19
  11.2 212.7 %all-gather.11.cloned.1.call-start = ((), (), s32[]{:S(2)}) async-start(), calls=%async_computation.1 | async-start | bytes 1179648 | tf_op jit(solution)/shard_map/all_gather | solution.py:18
  121.8 178.0 %all-gather.23.cloned.1.call-start = ((), (), s32[]{:S(2)}) async-start(), calls=%async_computation.7 | async-start | bytes 2162688 | tf_op jit(solution)/shard_map/all_gather | solution.py:23
  228.9 70.9 %all-to-all-start = ((f32[8,256,128]{2,1,0:T(8,128)}), f32[8,256,128]{2,1,0:T(8,128)S(1)}, u32[]{:S(2)}, u32[]{:S(2)}) async-start(f32[8,256,128]{2,1,0:T(8,128)} %stack.30), calls=%async_computation | async-start | bytes 2097152 | tf_op jit(solution)/shard_map/all_to_all | solution.py:21
  232.6 73.7 %copy-start.2 = (f32[1024,128]{1,0:T(8,128)S(1)}, f32[1024,128]{1,0:T(8,128)}, u32[]{:S(2)}) copy-start(f32[1024,128]{1,0:T(8,128)} %param.9) | copy-start | bytes 1572868
  232.6 101.1 %all-gather.15.cloned.1.call-start = ((), (), s32[]{:S(2)}) async-start(), calls=%async_computation.3 | async-start | bytes 1179648 | tf_op jit(solution)/shard_map/all_gather | solution.py:24
  299.8 6.8 %copy-start.1 = (f32[256,128]{1,0:T(8,128)S(1)}, f32[256,128]{1,0:T(8,128)}, u32[]{:S(2)}) copy-start(f32[256,128]{1,0:T(8,128)} %fusion.6) | copy-start | bytes 393220
  299.8 175.0 %copy-start = (f32[2048,128]{1,0:T(8,128)S(1)}, f32[2048,128]{1,0:T(8,128)}, u32[]{:S(2)}) copy-start(f32[2048,128]{1,0:T(8,128)} %all-gather.11.cloned.1.call-done) | copy-start | bytes 3145732
  305.6 169.2 %all-gather.17.cloned.1.call-start = ((), (), s32[]{:S(2)}) async-start(), calls=%async_computation.4 | async-start | bytes 17301504 | tf_op jit(solution)/shard_map/all_gather | solution.py:29
Sparse Core Ops, SparseCore 0:
  10.4 29.9 all-gather.20
  43.0 72.8 all-gather.18
  118.4 75.1 all-gather.12
  195.9 27.9 all-gather.10
  226.9 72.8 all-gather.22
  305.7 27.9 all-gather.14
  336.3 138.4 all-gather.16
